TPU v7x, 256 devices: a whole 4x4x8 slice. The times are simulated.
256 devices in a mesh: seq: 8 (over y, core), item: 32 (over z, x).
Axes of the slice: x: 4, y: 4, z: 8, core: 2. Of those that a mesh axis runs over, the one named last changes fastest.
Arguments:
- events: float32 [32, 1024, 512], P('item', 'seq'), may hold values from -6 to 6
- w_uvqk: float32 [512, 2048], replicated, may hold values from -0.25 to 0.25
- out_gain: float32 [512], replicated, may hold values from 0.5 to 1.5
- w_out: float32 [512, 512], replicated, may hold values from -0.25 to 0.25
- item_table: float32 [32768, 512], P('item'), may hold values from -0.25 to 0.25
- user_lengths: int32 [32, 4], P('item'), may hold values from 1 to 512, 1024 in all within a row
- neg_ids: int32 [4, 512], replicated, may hold values from 0 to 1023
- panel_owner: int32 [4], replicated, may hold values from 0 to 31
- block_mask: int32 [32, 8], P('item', 'seq'), may hold values from 1 to 65535
- targets: int32 [32, 1024], P('item', 'seq'), may hold values from 0 to 2047
Outputs:
- mean_loss: float32 [], replicated
- event_grad: float32 [32, 1024, 512], P('item', 'seq')
- table_grad: float32 [32768, 512], P('item')
Inputs may be any that keep to these rules, and one draw needn't show every extreme that they name: `user_lengths`: the 4 lengths of a group sum to 1024, the longest is exactly 512. `neg_ids`: rows may repeat within and across panels. `panel_owner`: several panels may have one owner. `block_mask`: bit k of an entry admits negative columns 128 k to 128 k + 127 for the 128 events of that block.
All inputs are finite; a program needn't handle non-finite values.
Results may differ from a plain program's by a relative error of at most 0.0003.
Values sent between devices are 32-bit elements; how exact they have to be, the bound alone decides.
A program may use at most 64 MiB of HBM per device.

v0:
```python
import jax
import jax.numpy as jnp
from jax import lax
from jax.sharding import PartitionSpec as P

H = 16
highest = lax.Precision.HIGHEST
beta_weight = 0.75
epsilon = 1e-05


def broadcast(shard, axis, root):
    mine = lax.axis_index(axis) == root
    return lax.psum(jnp.where(mine, shard, jnp.zeros_like(shard)), axis)


def user_index(lengths, positions):
    user_ends = jnp.cumsum(lengths)
    return jnp.sum((positions[:, None] >= user_ends[None, :]).astype(jnp.int32), axis=1)


def pointwise(query_rows, key_rows, value_rows, query_pos, key_pos, query_user, key_user):
    scores = jnp.einsum("qhd,khd->hqk", query_rows, key_rows, precision=highest)
    allowed = (query_user[:, None] == key_user[None, :]) & (query_pos[:, None] >= key_pos[None, :])
    weights = jax.nn.silu(scores) * allowed[None, :, :].astype(jnp.float32)
    return jnp.einsum("hqk,khd->qhd", weights, value_rows, precision=highest)


def loss_terms(outputs, negatives, mask_words, target_cols):
    logits = jnp.einsum("td,nd->tn", outputs, negatives, precision=highest)
    columns = jnp.arange(negatives.shape[0], dtype=jnp.int32)
    mask_bits = jnp.repeat(mask_words, 128)
    live_cols = jnp.bitwise_and(
        jnp.right_shift(mask_bits[:, None], columns[None, :] // 128), 1
    ).astype(jnp.float32)
    is_target = (columns[None, :] == target_cols[:, None]).astype(jnp.float32)
    neg_weight = live_cols * (1.0 - is_target)
    loss_part = jnp.sum(
        beta_weight * is_target * jax.nn.softplus(-logits) + neg_weight * jax.nn.softplus(logits)
    )
    grad_logits = neg_weight * jax.nn.sigmoid(logits) - beta_weight * is_target * jax.nn.sigmoid(
        -logits
    )
    grad_rows = jnp.dot(grad_logits, negatives, precision=highest)
    panel_part = jnp.einsum("tn,td->nd", grad_logits, outputs, precision=highest)
    return (loss_part, grad_rows, panel_part)


def per_device(
    events,
    w_uvqk,
    out_gain,
    w_out,
    item_table,
    user_lengths,
    neg_ids,
    panel_owner,
    block_mask,
    targets,
):
    rows_in = events[0]
    tok_rows, width = rows_in.shape
    head_size = width // H
    lengths = user_lengths[0]
    projected = jax.nn.silu(jnp.dot(rows_in, w_uvqk, precision=highest))
    gates_u = projected[:, :width]
    packed = projected[:, width:].reshape(tok_rows, 3, H, head_size)
    spread = lax.all_to_all(packed, "seq", split_axis=2, concat_axis=0, tiled=True)
    group_len = spread.shape[0]
    positions = jnp.arange(group_len, dtype=jnp.int32)
    user_ids = user_index(lengths, positions)
    block_rows = 512

    def one_block(first_row):
        query_rows = lax.dynamic_slice_in_dim(spread[:, 1], first_row, block_rows, 0)
        query_pos = first_row + jnp.arange(block_rows, dtype=jnp.int32)
        query_user = lax.dynamic_slice_in_dim(user_ids, first_row, block_rows, 0)
        return pointwise(
            query_rows, spread[:, 2], spread[:, 0], query_pos, positions, query_user, user_ids
        )

    firsts = jnp.arange(group_len // block_rows, dtype=jnp.int32) * block_rows
    attended = lax.map(one_block, firsts).reshape(group_len, spread.shape[2], head_size)
    attended = lax.all_to_all(attended, "seq", split_axis=0, concat_axis=1, tiled=True)
    attended = attended.reshape(tok_rows, width)
    row_mean = jnp.mean(attended, axis=1, keepdims=True)
    centered = attended - row_mean
    variance = jnp.mean(centered * centered, axis=1, keepdims=True)
    normed = centered * lax.rsqrt(variance + epsilon) * out_gain
    outputs = rows_in + jnp.dot(normed * gates_u, w_out, precision=highest)
    panel_list = []
    for panel_index in range(neg_ids.shape[0]):
        local_rows = item_table[neg_ids[panel_index]]
        panel_list.append(broadcast(local_rows, "item", panel_owner[panel_index]))
    negatives = jnp.concatenate(panel_list, axis=0)
    loss_part, grad_rows, panel_part = loss_terms(outputs, negatives, block_mask[0], targets[0])
    panel_total, loss_total = lax.psum((panel_part, loss_part), ("seq", "item"))
    owned_panels = (panel_owner == lax.axis_index("item")).astype(jnp.float32)
    owned_rows = jnp.repeat(owned_panels, neg_ids.shape[1])
    table_grad = (
        jnp.zeros_like(item_table).at[neg_ids.reshape(-1)].add(panel_total * owned_rows[:, None])
    )
    event_total = tok_rows * lax.axis_size("seq") * lax.axis_size("item")
    return (loss_total / event_total, grad_rows[None], table_grad)


def solution(mesh):
    placed = (
        P("item", "seq", None),
        P(),
        P(),
        P(),
        P("item", None),
        P("item", None),
        P(),
        P(),
        P("item", "seq"),
        P("item", "seq"),
    )
    return jax.shard_map(
        per_device,
        mesh=mesh,
        in_specs=placed,
        out_specs=(P(), P("item", "seq", None), P("item", None)),
        check_vma=False,
    )
```

profile of v0, /device:TPU:2, one launch (start us, length us, event | category | flops | bytes accessed | tf_op | source)
XLA Modules:
  0.0 512.6 jit_solution(2004496451884381589)
XLA Ops:
  7.2 4.8 divide_multiply_fusion
  16.3 4.5 all-to-all-start
  23.3 2.3 gather_fusion.1
  26.9 2.3 gather_fusion.2
  29.9 2.3 gather_fusion.3
  37.6 2.5 copy.29
  41.4 24.4 %while.11 = (s32[]{:T(128)}, f32[2,512,2,32]{1,3,2,0:T(8,128)S(1)}, f32[1024,3,2,32]{0,3,2,1:T(8,128)S(1)}, s32[2]{0:T(128)S(1)}, s32[1024]{0:T(1024)S(1)}, /*index=5*/s32[]{:T(128)}, s32[]{:T(128)}, s32[]{:T(128)}) while((s32[]{:T(128)}, f32[2,512,2,32]{1,3,2,0:T(8,128)S(1)}, f32[1024,3,2,32]{0,3,2,1:T(8,128)S(1)}, ...), condition=%wide.region_3.4_spmd.clone, body=%wide.region_2.3_spmd.clone.sunk | while | flops 812646912 | bytes 13908123 | solution.py:83
  44.0 3.6 fusion.75
  48.7 4.9 fusion.77
  56.2 3.6 fusion.75
  60.9 4.9 fusion.77
  66.6 1.8 reshape.354
  68.3 4.6 all-to-all-start.1
  73.6 6.8 %all-to-all-done.1 = f32[8,1,8192]{2,1,0:T(1,128)S(1)} async-done(((f32[8,1,8192]{2,1,0:T(1,128)}), f32[8,1,8192]{2,1,0:T(1,128)S(1)}, u32[]{:S(2)}, u32[]{:S(2)}) %all-to-all-start.1) | async-done | bytes 262176 | tf_op jit(solution)/shard_map/all_to_all | solution.py:84
  86.3 2.1 reduce_sum.44
  89.5 2.1 convolution_add_fusion
  91.6 112.1 %all-reduce.6.cloned.1.call-done = (f32[512,512]{1,0:T(8,128)}, f32[512,512]{1,0:T(8,128)}, f32[512,512]{1,0:T(8,128)}, f32[512,512]{1,0:T(8,128)}) async-done(((f32[512,512]{1,0:T(8,128)}, f32[512,512]{1,0:T(8,128)}, f32[512,512]{1,0:T(8,128)}, f32[512,512]{1,0:T(8,128)}), (f32[512,512]{1,0:T(8,128)}, f32[512,512]{1,0:T(8,128)}, f32[512,512]{1,0:T(8,128)}, ...) | async-done | bytes 4194320 | tf_op jit(solution)/shard_map/psum | solution.py:14
  206.6 2.0 copy-done.6
  208.6 6.1 %fusion.32 = (f32[]{:T(128)}, f32[128,2048]{1,0:T(8,128)S(1)}) fusion(f32[2048]{0:T(1024)S(1)} %fusion.50, s32[128]{0:T(128)S(1)} %bitcast.105, f32[128,512]{1,0:T(8,128)S(1)} %convolution_add_fusion, f32[2048,512]{1,0:T(8,128)S(1)} %constant_dynamic-update-slice_fusion), kind=kOutput, calls=%fused_computation.40 | convolution fusion | flops 1616379904 | bytes 5513732 | tf_op jit(solution)/shard_map/td,nd->tn/dot_general | solution.py:30
  214.7 5.4 %fusion.54 = f32[2048,512]{1,0:T(8,128)} fusion(f32[128,512]{1,0:T(8,128)S(1)} %convolution_add_fusion, f32[128,2048]{1,0:T(8,128)S(1)} %get-tuple-element.71, f32[2048]{0:T(1024)S(1)} %fusion.50, s32[128]{0:T(128)S(1)} %bitcast.106), kind=kOutput, calls=%fused_computation.95 | convolution fusion | flops 1614020608 | bytes 5513728 | tf_op jit(solution)/shard_map/tn,td->nd/dot_general | solution.py:45
  220.3 74.6 %psum.46 = f32[]{:T(128)} all-reduce(f32[]{:T(128)} %get-tuple-element.70), channel_id=1, replica_groups=mesh['seq'=8,'item'=32] {'seq','item'}, use_global_device_ids=true, to_apply=%region_12.13 | all-reduce | flops 1 | bytes 8 | tf_op jit(solution)/shard_map/psum | solution.py:97
  295.5 5.9 %convolution_bitcast_fusion = f32[1,128,512]{2,1,0:T(8,128)} fusion(f32[2048,512]{1,0:T(8,128)} %copy-done.6, f32[128,2048]{1,0:T(8,128)S(1)} %get-tuple-element.71, f32[2048]{0:T(1024)S(1)} %fusion.50, s32[128]{0:T(128)S(1)} %bitcast.107), kind=kOutput, calls=%fused_computation.37 | convolution fusion | flops 1614020608 | bytes 5513728 | tf_op jit(solution)/shard_map/dot_general | solution.py:44
  301.4 187.6 %all-reduce.4.cloned.1.call-done = f32[2048,512]{1,0:T(8,128)} async-done(((f32[2048,512]{1,0:T(8,128)}), f32[2048,512]{1,0:T(8,128)}) %all-reduce.4.cloned.1.call-update) | async-done | bytes 4194320 | tf_op jit(solution)/shard_map/psum | solution.py:97
  489.0 15.7 %scatter_custom_fusion = f32[1024,512]{1,0:T(8,128)} fusion(s32[2048]{0:T(1024)S(1)} %bitcast.98, f32[2048,512]{1,0:T(8,128)} %all-reduce.4.cloned.1.call-done, f32[2048]{0:T(1024)S(1)} %bitcast.95, f32[]{:T(128)} %constant.39.clone.1), kind=kCustom, calls=%fused_computation.30 | custom fusion | flops 2097152 | bytes 6299652 | tf_op jit(solution)/shard_map/scatter-add | solution.py:101
  (76 shorter events, 26.9 us)
Async XLA Ops:
  7.2 14.5 %copy-start = (f32[1024,512]{1,0:T(8,128)S(1)}, f32[1024,512]{1,0:T(8,128)}, u32[]{:S(2)}) copy-start(f32[1024,512]{1,0:T(8,128)} %param.16) | copy-start | bytes 6291460
  12.0 1.0 copy-start.3
  13.0 8.0 %copy-start.7 = (s32[4,512]{1,0:T(4,128)S(1)}, s32[4,512]{1,0:T(4,128)}, u32[]{:S(2)}) copy-start(s32[4,512]{1,0:T(4,128)} %param.18) | copy-start | bytes 24580
  13.0 8.0 %copy-start.8 = (s32[4]{0:T(128)S(1)}, s32[4]{0:T(128)}, u32[]{:S(2)}) copy-start(s32[4]{0:T(128)} %param.19) | copy-start | bytes 52
  16.3 21.4 %all-to-all-start = ((f32[128,3,16,32]{0,3,1,2:T(8,128)}), f32[128,3,16,32]{0,3,1,2:T(8,128)}, u32[]{:S(2)}, u32[]{:S(2)}) async-start(f32[128,3,16,32]{0,3,1,2:T(8,128)} %copy.28), calls=%async_computation | async-start | bytes 1572864 | tf_op jit(solution)/shard_map/all_to_all | solution.py:68
  20.7 182.9 %all-reduce.6.cloned.1.call-start = ((), (), s32[]{:S(2)}) async-start(), calls=%async_computation.3 | async-start | bytes 8388608 | tf_op jit(solution)/shard_map/psum | solution.py:14
  32.9 2.2 copy-start.1
  32.9 3.3 copy-start.2
  35.1 2.3 copy-start.10
  66.6 22.9 %copy-start.9 = (f32[512]{0:T(512)S(1)}, f32[512]{0:T(512)}, u32[]{:S(2)}) copy-start(f32[512]{0:T(512)} %param.14) | copy-start | bytes 6148
  68.3 12.1 %all-to-all-start.1 = ((f32[8,1,8192]{2,1,0:T(1,128)}), f32[8,1,8192]{2,1,0:T(1,128)S(1)}, u32[]{:S(2)}, u32[]{:S(2)}) async-start(f32[8,1,8192]{2,1,0:T(1,128)} %reshape.354), calls=%async_computation.1 | async-start | bytes 524288 | tf_op jit(solution)/shard_map/all_to_all | solution.py:84
  72.9 416.0 %all-reduce.4.cloned.1.call-start = ((), (), s32[]{:S(2)}) async-start(), calls=%async_computation.2 | async-start | bytes 8388608 | tf_op jit(solution)/shard_map/psum | solution.py:97
  203.7 2.8 copy-start.5
  203.7 2.8 copy-start.4
  203.7 4.9 copy-start.11
  206.6 2.0 copy-start.6
Sparse Core Ops, SparseCore 0:
  37.5 166.1 all-reduce.5
  220.3 268.6 all-reduce.3
where the time goes:
time: 513 us
  waiting for transfers between devices  306 us (60%)
  blocking collectives  74.6 us (15%)
  matrix products  41.3 us (8%)
  local copies, waits for them, and re-layouts  30.8 us (6%)
  other arithmetic  26.9 us (5%)
  between operations  19.3 us (4%)
  starting transfers between devices  9.29 us (2%)
    psum x1, waiting for transfers between devices, per_device(): panel_total, loss_total = lax.psum((panel_part, loss_part), ('seq', 'item'))  188 us
    psum x1, waiting for transfers between devices, broadcast(): return lax.psum(jnp.where(mine, shard, jnp.zeros_like(shard)), axis)  112 us
    psum x1, blocking collectives, per_device(): panel_total, loss_total = lax.psum((panel_part, loss_part), ('seq', 'item'))  74.6 us
    scatter-add x1, other arithmetic, per_device(): jnp.zeros_like(item_table).at[neg_ids.reshape(-1)]  15.7 us
  transfers between devices with their start and end apart: 4, of which 3 were waited for; matrix products, arithmetic and copies ran while one was open for 11% of the time, Pallas kernels for 0%

commit v1 on v0

--- a/solution.py
+++ b/solution.py
@@ -94,7 +94,7 @@
         panel_list.append(broadcast(local_rows, "item", panel_owner[panel_index]))
     negatives = jnp.concatenate(panel_list, axis=0)
     loss_part, grad_rows, panel_part = loss_terms(outputs, negatives, block_mask[0], targets[0])
-    panel_total, loss_total = lax.psum((panel_part, loss_part), ("seq", "item"))
+    panel_total, loss_total = lax.psum(lax.psum((panel_part, loss_part), "seq"), "item")
     owned_panels = (panel_owner == lax.axis_index("item")).astype(jnp.float32)
     owned_rows = jnp.repeat(owned_panels, neg_ids.shape[1])
     table_grad = (

time: 513 us -> 488 us (0.951)
  waiting for transfers between devices: 306 us -> 267 us
  blocking collectives: 74.6 us -> 87.2 us
    psum x1 -> x2, waiting for transfers between devices: 188 us -> 148 us  [the longest x1 75.7 us: per_device(): lax.psum((panel_part, loss_part), 'seq')]
    psum x1 -> x2, blocking collectives: 74.6 us -> 87.2 us  [the longest x1 72.4 us: per_device(): lax.psum(lax.psum((panel_part, loss_part), 'seq'), 'item')]
  transfers between devices with their start and end apart: 4 -> 5, of which waited for: 3 -> 4; matrix products, arithmetic and copies ran while one was open for 11% -> 12% of each run, Pallas kernels for 0% -> 0%
where the time goes in v1:
time: 488 us; the launch traced here: 486 us
  waiting for transfers between devices  267 us (55%)
  blocking collectives  87.2 us (18%)
  matrix products  41.3 us (8%)
  local copies, waits for them, and re-layouts  30.7 us (6%)
  other arithmetic  26.9 us (6%)
  between operations  19 us (4%)
  starting transfers between devices  9.34 us (2%)
    psum x1, waiting for transfers between devices, broadcast(): return lax.psum(jnp.where(mine, shard, jnp.zeros_like(shard)), axis)  112 us
    psum x1, waiting for transfers between devices, per_device(): lax.psum((panel_part, loss_part), 'seq')  75.7 us
    psum x1, waiting for transfers between devices, per_device(): lax.psum(lax.psum((panel_part, loss_part), 'seq'), 'item')  72.7 us
    psum x1, blocking collectives, per_device(): lax.psum(lax.psum((panel_part, loss_part), 'seq'), 'item')  72.4 us
    scatter-add x1, other arithmetic, per_device(): jnp.zeros_like(item_table).at[neg_ids.reshape(-1)]  15.7 us
    psum x1, blocking collectives, per_device(): lax.psum((panel_part, loss_part), 'seq')  14.8 us
  transfers between devices with their start and end apart: 5, of which 4 were waited for; matrix products, arithmetic and copies ran while one was open for 12% of the time, Pallas kernels for 0%

profile of v1, /device:TPU:2, one launch (start us, length us, event | category | flops | bytes accessed | tf_op | source)
XLA Modules:
  0.0 485.8 jit_solution(4994366870911141523)
XLA Ops:
  7.2 4.8 divide_multiply_fusion
  16.3 4.5 all-to-all-start
  23.3 2.3 gather_fusion.1
  26.9 2.3 gather_fusion.2
  29.9 2.3 gather_fusion.3
  37.6 2.5 copy.29
  41.4 24.4 %while.11 = (s32[]{:T(128)}, f32[2,512,2,32]{1,3,2,0:T(8,128)S(1)}, f32[1024,3,2,32]{0,3,2,1:T(8,128)S(1)}, s32[2]{0:T(128)S(1)}, s32[1024]{0:T(1024)S(1)}, /*index=5*/s32[]{:T(128)}, s32[]{:T(128)}, s32[]{:T(128)}) while((s32[]{:T(128)}, f32[2,512,2,32]{1,3,2,0:T(8,128)S(1)}, f32[1024,3,2,32]{0,3,2,1:T(8,128)S(1)}, ...), condition=%wide.region_3.4_spmd.clone, body=%wide.region_2.3_spmd.clone.sunk | while | flops 812646912 | bytes 13908123 | solution.py:83
  44.0 3.6 fusion.75
  48.7 4.9 %fusion.77 = f32[2,512,2,32]{1,3,2,0:T(8,128)S(1)} fusion(f32[2,512,2,32]{1,3,2,0:T(8,128)S(1)} %get-tuple-element.116, s32[]{:T(128)S(6)} %copy.44, f32[2,512,1024]{2,1,0:T(8,128)S(1)} %fusion.75, f32[512,1024]{1,0:T(8,128)S(1)} %fusion.76, f32[1024,3,2,32]{0,3,2,1:T(8,128)S(1)} %get-tuple-element.125), kind=kOutput, calls=%fused_computation.19.clone.1 | convolution fusion | flops 407896064 | bytes 6684676 | tf_op jit(solution)/shard_map/while/body/eval_jaxpr/hqk,khd->qhd/dot_general | solution.py:26
  56.2 3.6 fusion.75
  60.9 4.9 %fusion.77 = f32[2,512,2,32]{1,3,2,0:T(8,128)S(1)} fusion(f32[2,512,2,32]{1,3,2,0:T(8,128)S(1)} %get-tuple-element.116, s32[]{:T(128)S(6)} %copy.44, f32[2,512,1024]{2,1,0:T(8,128)S(1)} %fusion.75, f32[512,1024]{1,0:T(8,128)S(1)} %fusion.76, f32[1024,3,2,32]{0,3,2,1:T(8,128)S(1)} %get-tuple-element.125), kind=kOutput, calls=%fused_computation.19.clone.1 | convolution fusion | flops 407896064 | bytes 6684676 | tf_op jit(solution)/shard_map/while/body/eval_jaxpr/hqk,khd->qhd/dot_general | solution.py:26
  68.3 4.6 all-to-all-start.1
  73.6 6.8 %all-to-all-done.1 = f32[8,1,8192]{2,1,0:T(1,128)S(1)} async-done(((f32[8,1,8192]{2,1,0:T(1,128)}), f32[8,1,8192]{2,1,0:T(1,128)S(1)}, u32[]{:S(2)}, u32[]{:S(2)}) %all-to-all-start.1) | async-done | bytes 262176 | tf_op jit(solution)/shard_map/all_to_all | solution.py:84
  86.3 2.1 reduce_sum.44
  89.5 2.1 convolution_add_fusion
  91.6 112.1 %all-reduce.9.cloned.1.call-done = (f32[512,512]{1,0:T(8,128)}, f32[512,512]{1,0:T(8,128)}, f32[512,512]{1,0:T(8,128)}, f32[512,512]{1,0:T(8,128)}) async-done(((f32[512,512]{1,0:T(8,128)}, f32[512,512]{1,0:T(8,128)}, f32[512,512]{1,0:T(8,128)}, f32[512,512]{1,0:T(8,128)}), (f32[512,512]{1,0:T(8,128)}, f32[512,512]{1,0:T(8,128)}, f32[512,512]{1,0:T(8,128)}, ...) | async-done | bytes 4194320 | tf_op jit(solution)/shard_map/psum | solution.py:14
  208.5 6.1 %fusion.32 = (f32[]{:T(128)}, f32[128,2048]{1,0:T(8,128)S(1)}) fusion(f32[2048]{0:T(1024)S(1)} %fusion.50, s32[128]{0:T(128)S(1)} %bitcast.105, f32[128,512]{1,0:T(8,128)S(1)} %convolution_add_fusion, f32[2048,512]{1,0:T(8,128)S(1)} %constant_dynamic-update-slice_fusion), kind=kOutput, calls=%fused_computation.40 | convolution fusion | flops 1616379904 | bytes 5513732 | tf_op jit(solution)/shard_map/td,nd->tn/dot_general | solution.py:30
  214.6 5.4 %fusion.54 = f32[2048,512]{1,0:T(8,128)} fusion(f32[128,512]{1,0:T(8,128)S(1)} %convolution_add_fusion, f32[128,2048]{1,0:T(8,128)S(1)} %get-tuple-element.71, f32[2048]{0:T(1024)S(1)} %fusion.50, s32[128]{0:T(128)S(1)} %bitcast.106), kind=kOutput, calls=%fused_computation.95 | convolution fusion | flops 1614020608 | bytes 5513728 | tf_op jit(solution)/shard_map/tn,td->nd/dot_general | solution.py:45
  220.2 75.7 %all-reduce.5.cloned.1.call-done = f32[2048,512]{1,0:T(8,128)} async-done(((f32[2048,512]{1,0:T(8,128)}), f32[2048,512]{1,0:T(8,128)}) %all-reduce.5.cloned.1.call-update) | async-done | bytes 4194320 | tf_op jit(solution)/shard_map/psum | solution.py:97
  296.0 14.8 %psum.60 = f32[]{:T(128)} all-reduce(f32[]{:T(128)} %get-tuple-element.70), channel_id=1, replica_groups=mesh['seq'=8,'item'=32] {'seq'}, use_global_device_ids=true, to_apply=%region_12.13 | all-reduce | flops 1 | bytes 8 | tf_op jit(solution)/shard_map/psum | solution.py:97
  310.8 72.4 %psum.61 = f32[]{:T(128)} all-reduce(f32[]{:T(128)} %psum.60), channel_id=1, replica_groups=mesh['seq'=8,'item'=32] {'item'}, use_global_device_ids=true, to_apply=%region_13.14 | all-reduce | flops 1 | bytes 8 | tf_op jit(solution)/shard_map/psum | solution.py:97
  383.9 5.8 %convolution_bitcast_fusion = f32[1,128,512]{2,1,0:T(8,128)} fusion(f32[2048,512]{1,0:T(8,128)} %copy-done.6, f32[128,2048]{1,0:T(8,128)S(1)} %get-tuple-element.71, f32[2048]{0:T(1024)S(1)} %fusion.50, s32[128]{0:T(128)S(1)} %bitcast.107), kind=kOutput, calls=%fused_computation.37 | convolution fusion | flops 1614020608 | bytes 5513728 | tf_op jit(solution)/shard_map/dot_general | solution.py:44
  389.7 72.7 %all-reduce.7.cloned.1.call-done = f32[2048,512]{1,0:T(8,128)} async-done(((f32[2048,512]{1,0:T(8,128)}), f32[2048,512]{1,0:T(8,128)}) %all-reduce.7.cloned.1.call-update) | async-done | bytes 4194320 | tf_op jit(solution)/shard_map/psum | solution.py:97
  462.4 15.7 %scatter_custom_fusion = f32[1024,512]{1,0:T(8,128)} fusion(s32[2048]{0:T(1024)S(1)} %bitcast.98, f32[2048,512]{1,0:T(8,128)} %all-reduce.7.cloned.1.call-done, f32[2048]{0:T(1024)S(1)} %bitcast.95, f32[]{:T(128)} %constant.39.clone.1), kind=kCustom, calls=%fused_computation.30 | custom fusion | flops 2097152 | bytes 6299652 | tf_op jit(solution)/shard_map/scatter-add | solution.py:101
  (80 shorter events, 30.7 us)
Async XLA Ops:
  7.2 14.5 %copy-start = (f32[1024,512]{1,0:T(8,128)S(1)}, f32[1024,512]{1,0:T(8,128)}, u32[]{:S(2)}) copy-start(f32[1024,512]{1,0:T(8,128)} %param.16) | copy-start | bytes 6291460
  12.0 1.0 copy-start.3
  13.0 8.0 %copy-start.7 = (s32[4,512]{1,0:T(4,128)S(1)}, s32[4,512]{1,0:T(4,128)}, u32[]{:S(2)}) copy-start(s32[4,512]{1,0:T(4,128)} %param.18) | copy-start | bytes 24580
  13.0 8.0 %copy-start.8 = (s32[4]{0:T(128)S(1)}, s32[4]{0:T(128)}, u32[]{:S(2)}) copy-start(s32[4]{0:T(128)} %param.19) | copy-start | bytes 52
  16.3 21.4 %all-to-all-start = ((f32[128,3,16,32]{0,3,1,2:T(8,128)}), f32[128,3,16,32]{0,3,1,2:T(8,128)}, u32[]{:S(2)}, u32[]{:S(2)}) async-start(f32[128,3,16,32]{0,3,1,2:T(8,128)} %copy.28), calls=%async_computation | async-start | bytes 1572864 | tf_op jit(solution)/shard_map/all_to_all | solution.py:68
  20.7 182.9 %all-reduce.9.cloned.1.call-start = ((), (), s32[]{:S(2)}) async-start(), calls=%async_computation.4 | async-start | bytes 8388608 | tf_op jit(solution)/shard_map/psum | solution.py:14
  32.9 2.2 copy-start.1
  32.9 3.3 copy-start.2
  35.1 2.3 copy-start.10
  66.6 22.9 %copy-start.9 = (f32[512]{0:T(512)S(1)}, f32[512]{0:T(512)}, u32[]{:S(2)}) copy-start(f32[512]{0:T(512)} %param.14) | copy-start | bytes 6148
  68.3 12.1 %all-to-all-start.1 = ((f32[8,1,8192]{2,1,0:T(1,128)}), f32[8,1,8192]{2,1,0:T(1,128)S(1)}, u32[]{:S(2)}, u32[]{:S(2)}) async-start(f32[8,1,8192]{2,1,0:T(1,128)} %reshape.354), calls=%async_computation.1 | async-start | bytes 524288 | tf_op jit(solution)/shard_map/all_to_all | solution.py:84
  72.9 222.9 %all-reduce.5.cloned.1.call-start = ((), (), s32[]{:S(2)}) async-start(), calls=%async_computation.2 | async-start | bytes 8388608 | tf_op jit(solution)/shard_map/psum | solution.py:97
  203.7 2.8 copy-start.5
  203.7 2.8 copy-start.4
  203.7 4.8 copy-start.11
  206.6 1.9 copy-start.6
  220.1 242.3 %all-reduce.7.cloned.1.call-start = ((), (), s32[]{:S(2)}) async-start(), calls=%async_computation.3 | async-start | bytes 8388608 | tf_op jit(solution)/shard_map/psum | solution.py:97
Sparse Core Ops, SparseCore 0:
  37.5 166.1 all-reduce.8
  220.2 75.5 all-reduce.4
  299.4 162.9 all-reduce.6
